TPU v7x, 128 devices: a whole 4x4x4 slice. The times are simulated.
128 devices in a mesh: section: 8 (over x, z_hi), ctx: 16 (over z_lo, y, core).
Axes of the slice: x: 4, y: 4, z: 4 (z_hi: 2, z_lo: 2; z = z_hi * 2 + z_lo), core: 2. Of those that a mesh axis runs over, the one named last changes fastest.
Arguments:
- acts: bfloat16 [8, 2048, 12288], P('section', 'ctx'), may hold values from -6 to 6
- cots: bfloat16 [8, 2048, 4096], P('section', 'ctx'), may hold values from -1.1953125 to 1.1953125
- kern: float32 [8, 7, 12288], P('section'), may hold values from -2 to 2
- filt: bfloat16 [8, 4096, 2048], P('section', 'ctx'), may hold values from -9 to 9
- skip: float32 [8, 4096], P('section'), may hold values from 0.5 to 1.5
Outputs:
- output: bfloat16 [8, 2048, 4096], P('section', 'ctx')
- input_grad: bfloat16 [8, 2048, 12288], P('section', 'ctx')
- kern_grad: float32 [8, 7, 12288], P('section')
- filt_grad: float32 [8, 4096, 2048], P('section', 'ctx')
- skip_grad: float32 [8, 4096], P('section', 'ctx')
All inputs are finite; a program needn't handle non-finite values.
Results may differ from a plain program's by a relative error of at most 0.023.
Values may be sent and summed in bfloat16 or wider, within the bound.
No kernel may reach another device: no remote copies, remote signals or barrier semaphores. Data moves between devices by JAX's collectives and lax.ppermute only.
A program may use at most 192 MiB of HBM per device.

v0:
```python
import math
import jax
import jax.numpy as jnp
from jax import lax
from jax.sharding import PartitionSpec as P


def passed_along(value, axis, steps):
    count = lax.axis_size(axis)
    pairs = [(source, (source + steps) % count) for source in range(count)]
    return lax.ppermute(value, axis, pairs)


def from_behind(block, axis, distance):
    devices = range(lax.axis_size(axis))
    route = [(i - distance, i) for i in devices if i - distance in devices]
    return lax.ppermute(block, axis, route)


def factor_length(total):
    best = 2
    for divisor in range(2, math.isqrt(total) + 1):
        if total % divisor == 0 and divisor % 2 == 0:
            best = divisor
    return (best, total // best)


def phases(rows, cols, total):
    left = jnp.arange(rows, dtype=jnp.int32)[:, None]
    right = jnp.arange(cols, dtype=jnp.int32)[None, :]
    return (left * right % total).astype(jnp.float32) * (2.0 * math.pi / total)


def block_table(cos_t, sin_t, sign):
    top = jnp.stack([cos_t, sign * sin_t], axis=1)
    bottom = jnp.stack([-sign * sin_t, cos_t], axis=1)
    return jnp.stack([top, bottom], axis=0)


def make_tables(first, second):
    total = first * second
    outer = phases(first, first // 2, first)
    twist = phases(first, second, total)
    inner = phases(second, second, second)
    outer_pair = jnp.stack([jnp.cos(outer), -jnp.sin(outer)], axis=0)
    inner_cos = jnp.cos(inner)
    inner_sin = jnp.sin(inner)
    return (
        outer_pair,
        jnp.cos(twist),
        jnp.sin(twist),
        block_table(inner_cos, inner_sin, 1.0),
        block_table(inner_cos, inner_sin, -1.0),
    )


def contract(form, table, values):
    return jnp.einsum(form, table, values, precision=lax.Precision.HIGH)


def contract_narrow(form, table, values):
    upper = table.astype(jnp.bfloat16)
    lower = (table - upper.astype(jnp.float32)).astype(jnp.bfloat16)
    return jnp.einsum(form, upper, values, preferred_element_type=jnp.float32) + jnp.einsum(
        form, lower, values, preferred_element_type=jnp.float32
    )


def forward_transform(signal, tables):
    outer_pair, twist_cos, twist_sin, inner_fwd, inner_inv = tables
    first, second = twist_cos.shape
    columns = signal.shape[1]
    blocked = signal.reshape(first // 2, second, columns)
    spread = contract_narrow("pkm,mjc->pkjc", outer_pair, blocked)
    a_real = spread[0]
    a_imag = spread[1]
    b_real = a_real * twist_cos[:, :, None] + a_imag * twist_sin[:, :, None]
    b_imag = a_imag * twist_cos[:, :, None] - a_real * twist_sin[:, :, None]
    stacked = jnp.stack([b_real, b_imag], axis=0)
    return contract("pqsj,skjc->pkqc", inner_fwd, stacked)


def cmul(left, right, conj_right):
    if conj_right:
        return jnp.stack(
            [left[0] * right[0] + left[1] * right[1], left[1] * right[0] - left[0] * right[1]],
            axis=0,
        )
    return jnp.stack(
        [left[0] * right[0] - left[1] * right[1], left[0] * right[1] + left[1] * right[0]], axis=0
    )


def inverse_transform(spectrum, tables):
    outer_pair, twist_cos, twist_sin, inner_fwd, inner_inv = tables
    first, second = twist_cos.shape
    columns = spectrum.shape[3]
    back = contract("pjsq,skqc->pkjc", inner_inv, spectrum)
    g_real = back[0] * twist_cos[:, :, None] - back[1] * twist_sin[:, :, None]
    g_imag = back[0] * twist_sin[:, :, None] + back[1] * twist_cos[:, :, None]
    result = contract("skm,skjc->mjc", outer_pair, jnp.stack([g_real, g_imag], axis=0))
    return result.reshape(first // 2 * second, columns) / (first * second)


def on_device(acts, cots, kern, filt, skip):
    source = passed_along(acts, "section", 1)[0]
    incoming = passed_along(cots, "section", -1)[0]
    taps = kern.shape[1]
    margin = taps - 1
    tokens_dev, feats = source.shape
    width = feats // 3
    groups = lax.axis_size("ctx")
    chans = width // groups
    seq_len = tokens_dev * groups
    before = from_behind(source[tokens_dev - margin :], "ctx", 1)
    padded = jnp.concatenate([before, source], axis=0).astype(jnp.float32)
    weights = kern[0]
    feature = sum(
        (
            weights[offset][None, :] * padded[margin - offset : margin - offset + tokens_dev]
            for offset in range(taps)
        )
    )
    query = feature[:, :width]
    keyed = feature[:, width : 2 * width]
    value = feature[:, 2 * width :]
    gated = (keyed * value).astype(jnp.bfloat16)
    gain_all = skip[0]
    gain_part = lax.dynamic_slice_in_dim(gain_all, lax.axis_index("ctx") * chans, chans)
    first, second = factor_length(2 * seq_len)
    tables = make_tables(first, second)
    filt_spec = forward_transform(filt[0].T, tables)
    grad_in = incoming.astype(jnp.float32)
    grad_mix = (grad_in * query).astype(jnp.bfloat16)
    gated_part = lax.all_to_all(gated, "ctx", split_axis=1, concat_axis=0, tiled=True)
    gated_f = gated_part.astype(jnp.float32)
    gated_spec = forward_transform(gated_part, tables)
    mixed = inverse_transform(cmul(gated_spec, filt_spec, False), tables)
    mixed_part = mixed.astype(jnp.bfloat16)
    mixed_seq = lax.all_to_all(mixed_part, "ctx", split_axis=0, concat_axis=1, tiled=True)
    grad_part = lax.all_to_all(grad_mix, "ctx", split_axis=1, concat_axis=0, tiled=True)
    gated_f, gated_spec = (gated_f, gated_spec)
    grad_f = grad_part.astype(jnp.float32)
    grad_spec = forward_transform(grad_part, tables)
    back = inverse_transform(cmul(grad_spec, filt_spec, True), tables)
    filt_grad = inverse_transform(cmul(grad_spec, gated_spec, True), tables)
    through = (back + gain_part[None, :] * grad_f).astype(jnp.bfloat16)
    skip_grad = jnp.sum(grad_f * gated_f, axis=0)
    through_part, filt_grad, skip_grad = (through, filt_grad, skip_grad)
    through_seq = lax.all_to_all(through_part, "ctx", split_axis=0, concat_axis=1, tiled=True)
    inner = mixed_seq.astype(jnp.float32) + gain_all[None, :] * gated.astype(jnp.float32)
    output = (query * inner).astype(jnp.bfloat16)
    through_f = through_seq.astype(jnp.float32)
    feat_grad = jnp.concatenate([grad_in * inner, through_f * value, through_f * keyed], axis=1)
    after = from_behind(feat_grad[:margin].astype(jnp.bfloat16), "ctx", -1).astype(jnp.float32)
    extended = jnp.concatenate([feat_grad, after], axis=0)
    input_grad = sum(
        (
            weights[offset][None, :] * extended[offset : offset + tokens_dev]
            for offset in range(taps)
        )
    ).astype(jnp.bfloat16)
    partial_kern = jnp.sum(
        jnp.stack(
            [
                feat_grad * padded[margin - offset : margin - offset + tokens_dev]
                for offset in range(taps)
            ],
            axis=0,
        ),
        axis=1,
    )
    kern_grad = lax.psum(partial_kern.astype(jnp.bfloat16), "ctx").astype(jnp.float32)
    return (output[None], input_grad[None], kern_grad[None], filt_grad.T[None], skip_grad[None])


def solution(mesh):
    return jax.shard_map(
        on_device,
        mesh=mesh,
        in_specs=(
            P("section", "ctx", None),
            P("section", "ctx", None),
            P("section", None, None),
            P("section", "ctx", None),
            P("section", None),
        ),
        out_specs=(
            P("section", "ctx", None),
            P("section", "ctx", None),
            P("section", None, None),
            P("section", "ctx", None),
            P("section", "ctx"),
        ),
        check_vma=False,
    )
```

profile of v0, /device:TPU:25, one launch (start us, length us, event | category | flops | bytes accessed | tf_op | source)
XLA Modules:
  0.0 614.9 jit_solution(2262165847482371102)
XLA Ops:
  9.5 5.8 collective-permute-start.2
  15.3 4.6 copy.69
  22.4 82.2 %collective-permute-done = bf16[1,128,12288]{1,2,0:T(8,128)(2,1)} collective-permute-done((bf16[1,128,12288]{1,2,0:T(8,128)(2,1)}, bf16[1,128,12288]{1,2,0:T(8,128)(2,1)}, u32[]{:S(2)}, u32[]{:S(2)}) %collective-permute-start) | collective-permute-done | bytes 3145760 | tf_op jit(solution)/shard_map/ppermute | solution.py:11
  104.6 3.6 slice_bitcast_fusion
  108.2 3.9 copy.70
  117.6 3.6 copy.71
  121.3 4.7 maximum_convert_fusion
  126.1 24.5 %multiply_add_fusion = f32[128,12288]{0,1:T(8,128)} fusion(f32[134,12288]{0,1:T(8,128)S(1)} %maximum_convert_fusion, f32[12288]{0:T(1024)S(1)} %bitcast.243, f32[12288]{0:T(1024)S(1)} %bitcast.245, f32[12288]{0:T(1024)S(1)} %bitcast.235, f32[12288]{0:T(1024)S(1)} %bitcast.237, f32[12288]{0:T(1024)S(1)} %bitcast.239, f32[12288]{0:T(1024)S(1)} %bitcast.241, ...), kind=kLoop, calls=%fused_computation.60 | loop fusion | flops 20447232 | bytes 50675712 | tf_op jit(solution)/shard_map/add | solution.py:118
  153.8 7.0 %all-to-all-start.2 = ((bf16[128,16,256]{0,2,1:T(8,128)(2,1)}), bf16[128,16,256]{0,2,1:T(8,128)(2,1)S(1)}, u32[]{:S(2)}, u32[]{:S(2)}) async-start(bf16[128,16,256]{0,2,1:T(8,128)(2,1)} %bitcast.232), calls=%async_computation.2 | async-start | bytes 2097152 | tf_op jit(solution)/shard_map/all_to_all | solution.py:141
  162.1 4.6 convolution_add_fusion.1
  166.7 7.9 %all-to-all-done.2 = bf16[128,16,256]{0,2,1:T(8,128)(2,1)S(1)} async-done(((bf16[128,16,256]{0,2,1:T(8,128)(2,1)}), bf16[128,16,256]{0,2,1:T(8,128)(2,1)S(1)}, u32[]{:S(2)}, u32[]{:S(2)}) %all-to-all-start.2) | async-done | bytes 1048608 | tf_op jit(solution)/shard_map/all_to_all | solution.py:141
  178.8 7.3 %multiply_add_fusion.5 = (f32[1,64,64,256]{3,1,2,0:T(8,128)}, f32[1,64,64,256]{3,1,2,0:T(8,128)}, f32[1,64,64,256]{3,1,2,0:T(8,128)}, f32[1,64,64,256]{3,1,2,0:T(8,128)}) fusion(f32[2,64,64,256]{3,1,2,0:T(8,128)S(1)} %convolution_add_fusion, f32[64,64]{0,1:T(8,128)S(1)} %get-tuple-element.64, f32[64,64]{0,1:T(8,128)S(1)} %get-tuple-element.65, ...), kind=kLoop, calls=%fused_computation.70 | loop fusion | flops 12582912 | bytes 33587200 | tf_op jit(solution)/shard_map/add | solution.py:77
  186.1 4.1 maximum_bitcast_fusion.4
  190.2 4.1 maximum_bitcast_fusion.1
  194.3 8.5 %fusion.40 = f32[2,64,64,256]{3,2,0,1:T(8,128)S(1)} fusion(f32[2,64,64,256,1]{3,1,2,0,4:T(8,128)S(1)} %maximum_bitcast_fusion.4, f32[1,64,2,64]{3,1,2,0:T(8,128)S(1)} %get-tuple-element.57, f32[1,64,2,64]{3,1,2,0:T(8,128)S(1)} %get-tuple-element.60), kind=kOutput, calls=%fused_computation.84 | convolution fusion | flops 1610629120 | bytes 16842752 | tf_op jit(solution)/shard_map/pqsj,skjc->pkqc/dot_general | solution.py:58
  202.8 8.7 %fusion.37 = f32[2,64,64,256]{3,2,0,1:T(8,128)S(1)} fusion(f32[2,64,64,256,1]{3,1,2,0,4:T(8,128)S(1)} %maximum_bitcast_fusion.1, f32[1,64,2,64]{3,1,2,0:T(8,128)S(1)} %get-tuple-element.57, f32[1,64,2,64]{3,1,2,0:T(8,128)S(1)} %get-tuple-element.60), kind=kOutput, calls=%fused_computation.83 | convolution fusion | flops 1610629120 | bytes 16842752 | tf_op jit(solution)/shard_map/pqsj,skjc->pkqc/dot_general | solution.py:58
  211.5 4.7 multiply_add_fusion.4
  217.3 6.5 %fusion.44 = f32[64,256,2,64]{1,3,2,0:T(8,128)S(1)} fusion(f32[1,64,64,256]{3,2,0,1:T(8,128)} %get-tuple-element.23, f32[1,64,64,256]{3,2,0,1:T(8,128)} %get-tuple-element.22, f32[1,64,2,64]{3,1,2,0:T(8,128)S(1)} %get-tuple-element.61, f32[1,64,2,64]{3,1,2,0:T(8,128)S(1)} %get-tuple-element.56), kind=kOutput, calls=%fused_computation.86 | convolution fusion | flops 1612726272 | bytes 16842752 | tf_op jit(solution)/shard_map/pjsq,skqc->pkjc/dot_general | solution.py:58
  223.7 4.9 copy.164
  238.0 19.4 %all_to_all.52 = bf16[16,128,256]{1,2,0:T(8,128)(2,1)S(1)} all-to-all(bf16[16,128,256]{1,2,0:T(8,128)(2,1)S(1)} %fusion.48), channel_id=1, replica_groups=mesh['section'=8,'ctx'=16] {'ctx'}, dimensions={0} | all-to-all | bytes 2097152 | tf_op jit(solution)/shard_map/all_to_all | solution.py:150
  257.4 4.0 bitcast_multiply_fusion.4
  262.3 20.2 %all_to_all.53 = bf16[128,16,256]{0,2,1:T(8,128)(2,1)} all-to-all(bf16[128,16,256]{0,2,1:T(8,128)(2,1)S(1)} %bitcast.220), channel_id=1, replica_groups=mesh['section'=8,'ctx'=16] {'ctx'}, dimensions={1} | all-to-all | bytes 2097152 | tf_op jit(solution)/shard_map/all_to_all | solution.py:135
  290.1 4.2 maximum_bitcast_fusion
  294.3 14.0 %fusion.34 = f32[2,64,64,256]{3,2,0,1:T(8,128)} fusion(f32[2,64,64,256,1]{3,1,2,0,4:T(8,128)} %maximum_bitcast_fusion, f32[1,64,2,64]{3,1,2,0:T(8,128)S(1)} %get-tuple-element.57, f32[1,64,2,64]{3,1,2,0:T(8,128)S(1)} %get-tuple-element.60), kind=kOutput, calls=%fused_computation.82 | convolution fusion | flops 1610629120 | bytes 16842752 | tf_op jit(solution)/shard_map/pqsj,skjc->pkqc/dot_general | solution.py:58
  308.3 11.9 %multiply_add_fusion.2 = (f32[1,64,64,256]{3,2,0,1:T(8,128)}, f32[1,64,64,256]{3,2,0,1:T(8,128)}, f32[1,64,64,256]{3,2,0,1:T(8,128)}, f32[1,64,64,256]{3,2,0,1:T(8,128)}) fusion(f32[2,64,64,256]{3,2,0,1:T(8,128)S(1)} %bitcast.212, f32[2,64,64,256]{3,2,0,1:T(8,128)} %fusion.34, f32[2,64,64,256]{3,2,0,1:T(8,128)} %copy-done.8), kind=kLoop, calls=%fused_computation.64 | loop fusion | flops 12582912 | bytes 41943040 | tf_op jit(solution)/shard_map/add | solution.py:86
  320.1 6.4 %fusion.45 = f32[64,256,2,64]{1,3,2,0:T(8,128)S(1)} fusion(f32[1,64,64,256]{3,2,0,1:T(8,128)} %get-tuple-element.38, f32[1,64,64,256]{3,2,0,1:T(8,128)} %get-tuple-element.39, f32[1,64,2,64]{3,1,2,0:T(8,128)S(1)} %get-tuple-element.61, f32[1,64,2,64]{3,1,2,0:T(8,128)S(1)} %get-tuple-element.56), kind=kOutput, calls=%fused_computation.87 | convolution fusion | flops 1612726272 | bytes 16842752 | tf_op jit(solution)/shard_map/pjsq,skqc->pkjc/dot_general | solution.py:58
  326.6 4.9 copy.165
  331.4 6.5 %fusion.43 = f32[64,256,2,64]{1,3,2,0:T(8,128)S(1)} fusion(f32[1,64,64,256]{3,2,0,1:T(8,128)} %get-tuple-element.21, f32[1,64,64,256]{3,2,0,1:T(8,128)} %get-tuple-element.20, f32[1,64,2,64]{3,1,2,0:T(8,128)S(1)} %get-tuple-element.61, f32[1,64,2,64]{3,1,2,0:T(8,128)S(1)} %get-tuple-element.56), kind=kOutput, calls=%fused_computation.85 | convolution fusion | flops 1612726272 | bytes 16842752 | tf_op jit(solution)/shard_map/pjsq,skqc->pkjc/dot_general | solution.py:58
  337.9 8.2 %copy.163 = f32[64,256,2,64]{1,0,3,2:T(8,128)} copy(f32[64,256,2,64]{1,3,2,0:T(8,128)S(1)} %fusion.43) | data formatting | bytes 16777216 | tf_op jit(solution)/shard_map/pjsq,skqc->pkjc/dot_general | solution.py:58
  346.1 7.9 %multiply_subtract_fusion = (f32[1,64,64,256]{3,1,2,0:T(8,128)}, f32[1,64,64,256]{3,1,2,0:T(8,128)}, f32[1,64,64,256]{3,1,2,0:T(8,128)S(1)}, f32[1,64,64,256]{3,1,2,0:T(8,128)}) fusion(f32[2,64,64,256]{3,1,2,0:T(8,128)} %bitcast.217, f32[64,64]{0,1:T(8,128)S(1)} %get-tuple-element.64, f32[64,64]{0,1:T(8,128)S(1)} %get-tuple-element.65, ...), kind=kLoop, calls=%fused_computation.62 | loop fusion | flops 12582912 | bytes 33587200 | tf_op jit(solution)/shard_map/sub | solution.py:99
  353.9 5.1 fusion.51
  360.6 6.6 %all-to-all-start.1 = ((bf16[16,128,256]{2,1,0:T(8,128)(2,1)}), bf16[16,128,256]{2,1,0:T(8,128)(2,1)}, u32[]{:S(2)}, u32[]{:S(2)}) async-start(bf16[16,128,256]{2,1,0:T(8,128)(2,1)} %bitcast.231), calls=%async_computation.1 | async-start | bytes 2097152 | tf_op jit(solution)/shard_map/all_to_all | solution.py:140
  367.3 5.3 bitcast_multiply_fusion
  386.9 3.8 convert_multiply_fusion.1
  390.7 6.7 %pad_maximum_fusion.1 = bf16[128,12288]{0,1:T(8,128)(2,1)} fusion(f32[128,4096]{0,1:T(8,128)S(1)} %copy-done.1, f32[128,4096]{0,1:T(8,128)S(1)} %get-tuple-element.40, f32[128,4096]{0,1:T(8,128)S(1)} %get-tuple-element.43), kind=kLoop, calls=%fused_computation.52 | loop fusion | flops 9437184 | bytes 9437184 | tf_op jit(solution)/shard_map/concatenate | solution.py:154
  397.4 10.1 %bitcast_dynamic-update-slice_fusion.6 = f32[7,128,12288]{1,2,0:T(8,128)} fusion(f32[134,12288]{0,1:T(8,128)} %copy-done, f32[128,4096]{0,1:T(8,128)S(1)} %copy-done.1, f32[128,4096]{0,1:T(8,128)S(1)} %get-tuple-element.40, f32[128,4096]{0,1:T(8,128)S(1)} %get-tuple-element.43), kind=kLoop, calls=%fused_computation.59 | loop fusion | flops 4718591 | bytes 18874368
  412.9 10.0 %bitcast_dynamic-update-slice_fusion.5 = f32[7,128,12288]{1,2,0:T(8,128)} fusion(f32[7,128,12288]{1,2,0:T(8,128)} %bitcast_dynamic-update-slice_fusion.6, f32[134,12288]{0,1:T(8,128)} %copy-done, f32[128,4096]{0,1:T(8,128)} %get-tuple-element.41, f32[128,4096]{0,1:T(8,128)S(1)} %get-tuple-element.40, f32[128,4096]{0,1:T(8,128)} %copy-done.4), kind=kLoop, calls=%fused_computation.58 | loop fusion | flops 4718592 | bytes 18874368
  422.9 10.3 %bitcast_dynamic-update-slice_fusion.4 = f32[7,128,12288]{1,2,0:T(8,128)} fusion(f32[7,128,12288]{1,2,0:T(8,128)} %bitcast_dynamic-update-slice_fusion.5, f32[134,12288]{0,1:T(8,128)} %copy-done, f32[128,4096]{0,1:T(8,128)S(1)} %copy-done.2, f32[128,4096]{0,1:T(8,128)S(1)} %get-tuple-element.40, f32[128,4096]{0,1:T(8,128)S(1)} %copy-done.5), kind=kLoop, calls=%fused_computation.57 | loop fusion | flops 4718592 | bytes 18874368
  433.2 7.4 %bitcast_dynamic-update-slice_fusion.3 = f32[7,128,12288]{1,2,0:T(8,128)} fusion(f32[7,128,12288]{1,2,0:T(8,128)} %bitcast_dynamic-update-slice_fusion.4, f32[134,12288]{0,1:T(8,128)S(1)} %bitcast.210, f32[128,4096]{0,1:T(8,128)S(1)} %copy-done.2, f32[128,4096]{0,1:T(8,128)S(1)} %get-tuple-element.40, f32[128,4096]{0,1:T(8,128)S(1)} %copy-done.5), kind=kLoop, calls=%fused_computation.56 | loop fusion | flops 4718592 | bytes 18874368
  440.6 7.3 %bitcast_dynamic-update-slice_fusion.2 = f32[7,128,12288]{1,2,0:T(8,128)} fusion(f32[7,128,12288]{1,2,0:T(8,128)} %bitcast_dynamic-update-slice_fusion.3, f32[134,12288]{0,1:T(8,128)S(1)} %bitcast.210, f32[128,4096]{0,1:T(8,128)S(1)} %copy-done.2, f32[128,4096]{0,1:T(8,128)S(1)} %get-tuple-element.40, f32[128,4096]{0,1:T(8,128)S(1)} %copy-done.5), kind=kLoop, calls=%fused_computation.55 | loop fusion | flops 4718592 | bytes 18874368
  447.8 7.6 %bitcast_dynamic-update-slice_fusion.1 = f32[7,128,12288]{1,2,0:T(8,128)} fusion(f32[7,128,12288]{1,2,0:T(8,128)} %bitcast_dynamic-update-slice_fusion.2, f32[134,12288]{0,1:T(8,128)S(1)} %bitcast.210, f32[128,4096]{0,1:T(8,128)S(1)} %copy-done.2, f32[128,4096]{0,1:T(8,128)S(1)} %get-tuple-element.40, f32[128,4096]{0,1:T(8,128)S(1)} %copy-done.5), kind=kLoop, calls=%fused_computation.54 | loop fusion | flops 4718592 | bytes 18874368
  455.4 7.2 %bitcast_dynamic-update-slice_fusion = f32[7,128,12288]{1,2,0:T(8,128)} fusion(f32[7,128,12288]{1,2,0:T(8,128)} %bitcast_dynamic-update-slice_fusion.1, f32[134,12288]{0,1:T(8,128)S(1)} %bitcast.210, f32[128,4096]{0,1:T(8,128)S(1)} %copy-done.2, f32[128,4096]{0,1:T(8,128)S(1)} %get-tuple-element.40, f32[128,4096]{0,1:T(8,128)S(1)} %copy-done.5), kind=kLoop, calls=%fused_computation.53 | loop fusion | flops 4718592 | bytes 18874368 | tf_op jit(solution)/shard_map/stack | solution.py:164
  463.9 20.5 %reduce_sum.18 = bf16[7,12288]{1,0:T(8,128)(2,1)S(1)} reduce(f32[7,128,12288]{1,2,0:T(8,128)} %bitcast_dynamic-update-slice_fusion, f32[]{:T(128)} %constant.55.clone.1), dimensions={1}, to_apply=%region_0.1 | reduce | flops 10924032 | bytes 44212228 | tf_op jit(solution)/shard_map/reduce_sum | solution.py:163
  485.4 3.5 copy.94
  489.0 12.3 %pad_maximum_fusion = f32[134,12288]{0,1:T(8,128)} fusion(f32[6,12288]{0,1:T(8,128)} %copy.94, f32[128,4096]{0,1:T(8,128)} %get-tuple-element.41, f32[128,4096]{0,1:T(8,128)S(1)} %get-tuple-element.40, f32[128,4096]{0,1:T(8,128)} %copy-done.4), kind=kLoop, calls=%fused_computation | loop fusion | flops 4939776 | bytes 13172736 | tf_op jit(solution)/shard_map/concatenate | solution.py:156
  501.3 31.6 %fusion.46 = bf16[1,128,12288]{1,2,0:T(8,128)(2,1)} fusion(f32[134,12288]{0,1:T(8,128)} %pad_maximum_fusion, f32[12288]{0:T(1024)S(1)} %bitcast.244, f32[12288]{0:T(1024)S(1)} %bitcast.246, f32[12288]{0:T(1024)S(1)} %bitcast.236, f32[12288]{0:T(1024)S(1)} %bitcast.238, f32[12288]{0:T(1024)S(1)} %bitcast.240, f32[12288]{0:T(1024)S(1)} %bitcast.242, ...), kind=kLoop, calls=%fused_computation.89 | loop fusion | flops 25165824 | bytes 47529984 | tf_op jit(solution)/shard_map/broadcast_in_dim | solution.py:174
  532.9 4.6 copy.99
  537.5 68.2 %all-reduce.2.cloned.1.call-done = bf16[1,7,12288]{2,0,1:T(2,128)(2,1)} async-done(((bf16[1,7,12288]{2,0,1:T(2,128)(2,1)}), bf16[1,7,12288]{2,0,1:T(2,128)(2,1)}) %all-reduce.2.cloned.1.call-update) | async-done | bytes 172048 | tf_op jit(solution)/shard_map/psum | solution.py:173
  (123 shorter events, 63.6 us)
Async XLA Ops:
  7.2 14.5 %copy-start.29 = (f32[1,7,12288]{2,0,1:T(1,128)S(1)}, f32[1,7,12288]{2,0,1:T(1,128)}, u32[]{:S(2)}) copy-start(f32[1,7,12288]{2,0,1:T(1,128)} %param.7) | copy-start | bytes 1032196
  9.5 141.1 %collective-permute-start.2 = (bf16[1,128,4096]{1,2,0:T(8,128)(2,1)}, bf16[1,128,4096]{1,2,0:T(8,128)(2,1)S(1)}, u32[]{:S(2)}, u32[]{:S(2)}) collective-permute-start(bf16[1,128,4096]{1,2,0:T(8,128)(2,1)} %copy.84), channel_id=1, source_target_pairs={{0,112},{16,0},{32,16},{48,32},{64,48},{80,64},{96,80},{112,96},{1... | collective-permute-start | bytes 3145736 | tf_op jit(solution)/shard_map/ppermute | solution.py:11
  19.9 96.0 %copy-start.14 = (bf16[1,256,2048]{2,1,0:T(8,128)(2,1)S(1)}, bf16[1,256,2048]{2,1,0:T(8,128)(2,1)}, u32[]{:S(2)}) copy-start(bf16[1,256,2048]{2,1,0:T(8,128)(2,1)} %param.8) | copy-start | bytes 3145732
  19.9 84.7 %collective-permute-start = (bf16[1,128,12288]{1,2,0:T(8,128)(2,1)}, bf16[1,128,12288]{1,2,0:T(8,128)(2,1)}, u32[]{:S(2)}, u32[]{:S(2)}) collective-permute-start(bf16[1,128,12288]{1,2,0:T(8,128)(2,1)} %copy.69), channel_id=1, source_target_pairs={{0,16},{16,32},{32,48},{48,64},{64,80},{80,96},{96,112},{112,0},{1... | collective-permute-start | bytes 9437192 | tf_op jit(solution)/shard_map/ppermute | solution.py:11
  22.4 103.6 %copy-start.15 = (f32[1,1,12288]{2,0,1:T(1,128)}, f32[1,1,12288]{2,0,1:T(1,128)S(1)}, u32[]{:S(2)}) copy-start(f32[1,1,12288]{2,0,1:T(1,128)S(1)} %get-tuple-element.45) | copy-start | bytes 147460
  112.0 5.6 collective-permute-start.1
  121.2 4.8 copy-start.17
  121.2 4.8 copy-start.19
  121.2 4.8 copy-start.21
  121.2 4.8 copy-start.23
  121.2 4.8 copy-start.25
  121.2 4.8 copy-start.27
  126.0 24.6 %copy-start = (f32[134,12288]{0,1:T(8,128)}, f32[134,12288]{0,1:T(8,128)S(1)}, u32[]{:S(2)}) copy-start(f32[134,12288]{0,1:T(8,128)S(1)} %maximum_convert_fusion) | copy-start | bytes 19759108
  150.6 11.4 %copy-start.13 = (bf16[1,128,4096]{1,2,0:T(8,128)(2,1)}, bf16[1,128,4096]{1,2,0:T(8,128)(2,1)S(1)}, u32[]{:S(2)}) copy-start(bf16[1,128,4096]{1,2,0:T(8,128)(2,1)S(1)} %collective-permute-done.2) | copy-start | bytes 3145732
  153.8 20.8 %all-to-all-start.2 = ((bf16[128,16,256]{0,2,1:T(8,128)(2,1)}), bf16[128,16,256]{0,2,1:T(8,128)(2,1)S(1)}, u32[]{:S(2)}, u32[]{:S(2)}) async-start(bf16[128,16,256]{0,2,1:T(8,128)(2,1)} %bitcast.232), calls=%async_computation.2 | async-start | bytes 2097152 | tf_op jit(solution)/shard_map/all_to_all | solution.py:141
  175.1 2.6 slice-start.5
  176.4 2.4 slice-start.6
  202.8 8.7 %copy-start.7 = (f32[2,64,64,256]{3,2,0,1:T(8,128)}, f32[2,64,64,256]{3,2,0,1:T(8,128)S(1)}, u32[]{:S(2)}) copy-start(f32[2,64,64,256]{3,2,0,1:T(8,128)S(1)} %fusion.40) | copy-start | bytes 25165828
  211.5 5.8 copy-start.8
  233.1 4.5 copy-start.31
  261.3 1.0 copy-start.9
  284.7 2.6 copy-start.11
  290.1 18.2 %slice-start.3 = ((s8[8388608]{0:T(1024)(128)(4,1)}), s8[4194304]{0:T(1024)(128)(4,1)S(1)}, s32[]{:S(2)}) async-start(s8[8388608]{0:T(1024)(128)(4,1)} %bitcast.211), calls=%async_computation.8 | async-start | bytes 8388608
  294.3 14.0 %slice-start.4 = ((s8[8388608]{0:T(1024)(128)(4,1)}), s8[4194304]{0:T(1024)(128)(4,1)S(1)}, s32[]{:S(2)}) async-start(s8[8388608]{0:T(1024)(128)(4,1)} %bitcast.211), calls=%async_computation.9 | async-start | bytes 8388608
  360.6 20.5 %all-to-all-start.1 = ((bf16[16,128,256]{2,1,0:T(8,128)(2,1)}), bf16[16,128,256]{2,1,0:T(8,128)(2,1)}, u32[]{:S(2)}, u32[]{:S(2)}) async-start(bf16[16,128,256]{2,1,0:T(8,128)(2,1)} %bitcast.231), calls=%async_computation.1 | async-start | bytes 2097152 | tf_op jit(solution)/shard_map/all_to_all | solution.py:140
  367.3 238.5 %all-reduce.2.cloned.1.call-start = ((), (), s32[]{:S(2)}) async-start(), calls=%async_computation.4 | async-start | bytes 688128 | tf_op jit(solution)/shard_map/psum | solution.py:173
  375.1 11.7 %copy-start.30 = (f32[1,4096]{1,0:T(1,128)S(1)}, f32[1,4096]{1,0:T(1,128)}, u32[]{:S(2)}) copy-start(f32[1,4096]{1,0:T(1,128)} %param.9) | copy-start | bytes 49156
  380.2 6.7 %copy-start.10 = (bf16[128,4096]{0,1:T(8,128)(2,1)S(1)}, bf16[128,4096]{0,1:T(8,128)(2,1)}, u32[]{:S(2)}) copy-start(bf16[128,4096]{0,1:T(8,128)(2,1)} %copy-done.9) | copy-start | bytes 3145732
  386.9 3.8 copy-start.1
  390.7 16.8 %copy-start.4 = (f32[128,4096]{0,1:T(8,128)}, f32[128,4096]{0,1:T(8,128)S(1)}, u32[]{:S(2)}) copy-start(f32[128,4096]{0,1:T(8,128)S(1)} %get-tuple-element.43) | copy-start | bytes 6291460
  410.7 12.2 %copy-start.2 = (f32[128,4096]{0,1:T(8,128)S(1)}, f32[128,4096]{0,1:T(8,128)}, u32[]{:S(2)}) copy-start(f32[128,4096]{0,1:T(8,128)} %get-tuple-element.41) | copy-start | bytes 6291460
  410.7 12.2 %copy-start.5 = (f32[128,4096]{0,1:T(8,128)S(1)}, f32[128,4096]{0,1:T(8,128)}, u32[]{:S(2)}) copy-start(f32[128,4096]{0,1:T(8,128)} %copy-done.4) | copy-start | bytes 6291460
  410.7 74.7 %collective-permute-start.3 = (bf16[6,12288]{1,0:T(8,128)(2,1)S(1)}, bf16[6,12288]{1,0:T(8,128)(2,1)S(1)}, u32[]{:S(2)}, u32[]{:S(2)}) collective-permute-start(bf16[6,12288]{1,0:T(8,128)(2,1)S(1)} %copy.93), channel_id=1, source_target_pairs={{1,0},{2,1},{3,2},{4,3},{5,4},{6,5},{7,6},{8,7},{9,8},{10,9},{11,1... | collective-permute-start | bytes 442376 | tf_op jit(solution)/shard_map/ppermute | solution.py:17
  412.9 20.3 %slice-start = ((s8[12582912]{0:T(1024)(128)(4,1)}), s8[4194304]{0:T(1024)(128)(4,1)S(1)}, s32[]{:S(2)}) async-start(s8[12582912]{0:T(1024)(128)(4,1)} %bitcast.209), calls=%async_computation.5 | async-start | bytes 8388608
  412.9 20.3 %slice-start.1 = ((s8[12582912]{0:T(1024)(128)(4,1)}), s8[4194304]{0:T(1024)(128)(4,1)S(1)}, s32[]{:S(2)}) async-start(s8[12582912]{0:T(1024)(128)(4,1)} %bitcast.209), calls=%async_computation.6 | async-start | bytes 8388608
  422.9 10.3 %slice-start.2 = ((s8[12582912]{0:T(1024)(128)(4,1)}), s8[4194304]{0:T(1024)(128)(4,1)S(1)}, s32[]{:S(2)}) async-start(s8[12582912]{0:T(1024)(128)(4,1)} %bitcast.209), calls=%async_computation.7 | async-start | bytes 8388608
  455.4 7.2 %copy-start.12 = (bf16[128,4096]{0,1:T(8,128)(2,1)S(1)}, bf16[128,4096]{0,1:T(8,128)(2,1)}, u32[]{:S(2)}) copy-start(bf16[128,4096]{0,1:T(8,128)(2,1)} %get-tuple-element.44) | copy-start | bytes 3145732
  488.9 12.3 %copy-start.3 = (f32[128,4096]{0,1:T(8,128)S(1)}, f32[128,4096]{0,1:T(8,128)}, u32[]{:S(2)}) copy-start(f32[128,4096]{0,1:T(8,128)} %get-tuple-element.41) | copy-start | bytes 6291460
  488.9 12.3 %copy-start.6 = (f32[128,4096]{0,1:T(8,128)S(1)}, f32[128,4096]{0,1:T(8,128)}, u32[]{:S(2)}) copy-start(f32[128,4096]{0,1:T(8,128)} %copy-done.4) | copy-start | bytes 6291460
  488.9 12.3 %copy-start.16 = (f32[1,1,12288]{2,0,1:T(1,128)S(1)}, f32[1,1,12288]{2,0,1:T(1,128)}, u32[]{:S(2)}) copy-start(f32[1,1,12288]{2,0,1:T(1,128)} %copy-done.15) | copy-start | bytes 147460
  488.9 12.3 %copy-start.18 = (f32[1,1,12288]{2,0,1:T(1,128)S(1)}, f32[1,1,12288]{2,0,1:T(1,128)}, u32[]{:S(2)}) copy-start(f32[1,1,12288]{2,0,1:T(1,128)} %get-tuple-element.46) | copy-start | bytes 147460
  488.9 12.3 %copy-start.20 = (f32[1,1,12288]{2,0,1:T(1,128)S(1)}, f32[1,1,12288]{2,0,1:T(1,128)}, u32[]{:S(2)}) copy-start(f32[1,1,12288]{2,0,1:T(1,128)} %get-tuple-element.47) | copy-start | bytes 147460
  488.9 12.3 %copy-start.22 = (f32[1,1,12288]{2,0,1:T(1,128)S(1)}, f32[1,1,12288]{2,0,1:T(1,128)}, u32[]{:S(2)}) copy-start(f32[1,1,12288]{2,0,1:T(1,128)} %get-tuple-element.48) | copy-start | bytes 147460
  488.9 12.3 %copy-start.24 = (f32[1,1,12288]{2,0,1:T(1,128)S(1)}, f32[1,1,12288]{2,0,1:T(1,128)}, u32[]{:S(2)}) copy-start(f32[1,1,12288]{2,0,1:T(1,128)} %get-tuple-element.49) | copy-start | bytes 147460
  488.9 12.3 %copy-start.26 = (f32[1,1,12288]{2,0,1:T(1,128)S(1)}, f32[1,1,12288]{2,0,1:T(1,128)}, u32[]{:S(2)}) copy-start(f32[1,1,12288]{2,0,1:T(1,128)} %get-tuple-element.50) | copy-start | bytes 147460
  488.9 12.3 %copy-start.28 = (f32[1,1,12288]{2,0,1:T(1,128)S(1)}, f32[1,1,12288]{2,0,1:T(1,128)}, u32[]{:S(2)}) copy-start(f32[1,1,12288]{2,0,1:T(1,128)} %get-tuple-element.51) | copy-start | bytes 147460
Sparse Core Ops, SparseCore 0:
  485.5 120.2 all-reduce.1
where the time goes:
time: 625 us; the launch traced here: 615 us
  other arithmetic  228 us (36%)
  waiting for transfers between devices  160 us (26%)
  matrix products  76.2 us (12%)
  local copies, waits for them, and re-layouts  72.4 us (12%)
  blocking collectives  39.5 us (6%)
  starting transfers between devices  24.3 us (4%)
  between operations  14.9 us (2%)
    ppermute x2, waiting for transfers between devices, passed_along(): return lax.ppermute(value, axis, pairs)  82.2 us
    psum x1, waiting for transfers between devices, on_device(): lax.psum(partial_kern.astype(jnp.bfloat16), 'ctx').astype(jnp.float32)  68.2 us
    dot_general x9, matrix products, contract(): return jnp.einsum(form, table, values, precision=lax.Precision.HIGH)  63.9 us
    unnamed x9, other arithmetic  52.6 us
    broadcast_in_dim x1, other arithmetic, on_device(): input_grad[None]  31.6 us
    add x1, other arithmetic, on_device(): sum((weights[offset][None, :] * padded[margin - offset:margin - offset +...  24.5 us
    reduce_sum x1, other arithmetic, on_device(): jnp.sum(jnp.stack([feat_grad * padded[margin - offset:margin - offset + t...  20.5 us
    all_to_all x1, blocking collectives, on_device(): lax.all_to_all(gated, 'ctx', split_axis=1, concat_axis=0, tiled=True)  20.2 us
  transfers between devices with their start and end apart: 7, of which 5 were waited for; matrix products, arithmetic and copies ran while one was open for 31% of the time, Pallas kernels for 0%

commit v1 on v0

--- a/solution.py
+++ b/solution.py
@@ -170,7 +170,9 @@
         ),
         axis=1,
     )
-    kern_grad = lax.psum(partial_kern.astype(jnp.bfloat16), "ctx").astype(jnp.float32)
+    kern_grad = jnp.sum(lax.all_gather(partial_kern.astype(jnp.bfloat16), "ctx"), axis=0).astype(
+        jnp.float32
+    )
     return (output[None], input_grad[None], kern_grad[None], filt_grad.T[None], skip_grad[None])
 
 

time: 625 us -> 565 us (0.904)
  the two profiles are of different devices: /device:TPU:25 before, /device:TPU:71 now
where the time goes in v1:
time: 565 us; the launch traced here: 556 us
  other arithmetic  226 us (40%)
  waiting for transfers between devices  103 us (18%)
  matrix products  76.2 us (13%)
  local copies, waits for them, and re-layouts  73.3 us (13%)
  blocking collectives  38.9 us (7%)
  starting transfers between devices  23.3 us (4%)
  between operations  14.8 us (3%)
    ppermute x2, waiting for transfers between devices, passed_along(): return lax.ppermute(value, axis, pairs)  84.2 us
    dot_general x9, matrix products, contract(): return jnp.einsum(form, table, values, precision=lax.Precision.HIGH)  63.9 us
    unnamed x9, other arithmetic  48.5 us
    broadcast_in_dim x1, other arithmetic, on_device(): input_grad[None]  32.3 us
    add x1, other arithmetic, on_device(): sum((weights[offset][None, :] * padded[margin - offset:margin - offset +...  24.5 us
    reduce_sum x1, other arithmetic, on_device(): jnp.sum(jnp.stack([feat_grad * padded[margin - offset:margin - offset + t...  21.1 us
    unnamed x76, local copies, waits for them, and re-layouts  20.5 us
    all_to_all x1, blocking collectives, on_device(): lax.all_to_all(gated, 'ctx', split_axis=1, concat_axis=0, tiled=True)  20.2 us
  transfers between devices with their start and end apart: 7, of which 5 were waited for; matrix products, arithmetic and copies ran while one was open for 24% of the time, Pallas kernels for 0%

profile of v1, /device:TPU:71, one launch (start us, length us, event | category | flops | bytes accessed | tf_op | source)
XLA Modules:
  0.0 555.6 jit_solution(8301956620550157155)
XLA Ops:
  9.5 4.6 copy.69
  14.1 5.1 collective-permute-start
  21.7 84.2 %collective-permute-done = bf16[1,128,12288]{1,2,0:T(8,128)(2,1)} collective-permute-done((bf16[1,128,12288]{1,2,0:T(8,128)(2,1)}, bf16[1,128,12288]{1,2,0:T(8,128)(2,1)}, u32[]{:S(2)}, u32[]{:S(2)}) %collective-permute-start) | collective-permute-done | bytes 3145760 | tf_op jit(solution)/shard_map/ppermute | solution.py:11
  105.9 3.6 slice_bitcast_fusion
  109.5 3.9 copy.70
  113.3 3.6 collective-permute-start.1
  119.8 3.6 copy.71
  123.5 4.7 maximum_convert_fusion
  128.3 24.5 %multiply_add_fusion = f32[128,12288]{0,1:T(8,128)} fusion(f32[134,12288]{0,1:T(8,128)S(1)} %maximum_convert_fusion, f32[12288]{0:T(1024)S(1)} %bitcast.247, f32[12288]{0:T(1024)S(1)} %bitcast.249, f32[12288]{0:T(1024)S(1)} %bitcast.239, f32[12288]{0:T(1024)S(1)} %bitcast.241, f32[12288]{0:T(1024)S(1)} %bitcast.243, f32[12288]{0:T(1024)S(1)} %bitcast.245, ...), kind=kLoop, calls=%fused_computation.60 | loop fusion | flops 20447232 | bytes 50675712 | tf_op jit(solution)/shard_map/add | solution.py:118
  156.0 6.8 %all-to-all-start.2 = ((bf16[128,16,256]{0,2,1:T(8,128)(2,1)}), bf16[128,16,256]{0,2,1:T(8,128)(2,1)S(1)}, u32[]{:S(2)}, u32[]{:S(2)}) async-start(bf16[128,16,256]{0,2,1:T(8,128)(2,1)} %bitcast.235), calls=%async_computation.2 | async-start | bytes 2097152 | tf_op jit(solution)/shard_map/all_to_all | solution.py:141
  164.1 4.6 convolution_add_fusion.1
  168.7 10.0 %all-to-all-done.2 = bf16[128,16,256]{0,2,1:T(8,128)(2,1)S(1)} async-done(((bf16[128,16,256]{0,2,1:T(8,128)(2,1)}), bf16[128,16,256]{0,2,1:T(8,128)(2,1)S(1)}, u32[]{:S(2)}, u32[]{:S(2)}) %all-to-all-start.2) | async-done | bytes 1048608 | tf_op jit(solution)/shard_map/all_to_all | solution.py:141
  182.9 7.3 %multiply_add_fusion.5 = (f32[1,64,64,256]{3,1,2,0:T(8,128)}, f32[1,64,64,256]{3,1,2,0:T(8,128)}, f32[1,64,64,256]{3,1,2,0:T(8,128)}, f32[1,64,64,256]{3,1,2,0:T(8,128)}) fusion(f32[2,64,64,256]{3,1,2,0:T(8,128)S(1)} %convolution_add_fusion, f32[64,64]{0,1:T(8,128)S(1)} %get-tuple-element.64, f32[64,64]{0,1:T(8,128)S(1)} %get-tuple-element.65, ...), kind=kLoop, calls=%fused_computation.70 | loop fusion | flops 12582912 | bytes 33587200 | tf_op jit(solution)/shard_map/add | solution.py:77
  190.2 4.1 maximum_bitcast_fusion.4
  194.3 4.1 maximum_bitcast_fusion.1
  198.4 8.5 %fusion.40 = f32[2,64,64,256]{3,2,0,1:T(8,128)S(1)} fusion(f32[2,64,64,256,1]{3,1,2,0,4:T(8,128)S(1)} %maximum_bitcast_fusion.4, f32[1,64,2,64]{3,1,2,0:T(8,128)S(1)} %get-tuple-element.57, f32[1,64,2,64]{3,1,2,0:T(8,128)S(1)} %get-tuple-element.60), kind=kOutput, calls=%fused_computation.84 | convolution fusion | flops 1610629120 | bytes 16842752 | tf_op jit(solution)/shard_map/pqsj,skjc->pkqc/dot_general | solution.py:58
  206.9 8.7 %fusion.37 = f32[2,64,64,256]{3,2,0,1:T(8,128)S(1)} fusion(f32[2,64,64,256,1]{3,1,2,0,4:T(8,128)S(1)} %maximum_bitcast_fusion.1, f32[1,64,2,64]{3,1,2,0:T(8,128)S(1)} %get-tuple-element.57, f32[1,64,2,64]{3,1,2,0:T(8,128)S(1)} %get-tuple-element.60), kind=kOutput, calls=%fused_computation.83 | convolution fusion | flops 1610629120 | bytes 16842752 | tf_op jit(solution)/shard_map/pqsj,skjc->pkqc/dot_general | solution.py:58
  215.6 4.7 multiply_add_fusion.4
  221.4 6.5 %fusion.44 = f32[64,256,2,64]{1,3,2,0:T(8,128)S(1)} fusion(f32[1,64,64,256]{3,2,0,1:T(8,128)} %get-tuple-element.23, f32[1,64,64,256]{3,2,0,1:T(8,128)} %get-tuple-element.22, f32[1,64,2,64]{3,1,2,0:T(8,128)S(1)} %get-tuple-element.61, f32[1,64,2,64]{3,1,2,0:T(8,128)S(1)} %get-tuple-element.56), kind=kOutput, calls=%fused_computation.86 | convolution fusion | flops 1612726272 | bytes 16842752 | tf_op jit(solution)/shard_map/pjsq,skqc->pkjc/dot_general | solution.py:58
  227.9 4.9 copy.164
  242.1 18.8 %all_to_all.52 = bf16[16,128,256]{1,2,0:T(8,128)(2,1)S(1)} all-to-all(bf16[16,128,256]{1,2,0:T(8,128)(2,1)S(1)} %fusion.48), channel_id=1, replica_groups=mesh['section'=8,'ctx'=16] {'ctx'}, dimensions={0} | all-to-all | bytes 2097152 | tf_op jit(solution)/shard_map/all_to_all | solution.py:150
  260.9 4.0 bitcast_multiply_fusion.4
  265.8 20.2 %all_to_all.53 = bf16[128,16,256]{0,2,1:T(8,128)(2,1)} all-to-all(bf16[128,16,256]{0,2,1:T(8,128)(2,1)S(1)} %bitcast.223), channel_id=1, replica_groups=mesh['section'=8,'ctx'=16] {'ctx'}, dimensions={1} | all-to-all | bytes 2097152 | tf_op jit(solution)/shard_map/all_to_all | solution.py:135
  293.7 4.2 maximum_bitcast_fusion
  297.8 14.0 %fusion.34 = f32[2,64,64,256]{3,2,0,1:T(8,128)} fusion(f32[2,64,64,256,1]{3,1,2,0,4:T(8,128)} %maximum_bitcast_fusion, f32[1,64,2,64]{3,1,2,0:T(8,128)S(1)} %get-tuple-element.57, f32[1,64,2,64]{3,1,2,0:T(8,128)S(1)} %get-tuple-element.60), kind=kOutput, calls=%fused_computation.82 | convolution fusion | flops 1610629120 | bytes 16842752 | tf_op jit(solution)/shard_map/pqsj,skjc->pkqc/dot_general | solution.py:58
  311.8 11.9 %multiply_add_fusion.2 = (f32[1,64,64,256]{3,2,0,1:T(8,128)}, f32[1,64,64,256]{3,2,0,1:T(8,128)}, f32[1,64,64,256]{3,2,0,1:T(8,128)}, f32[1,64,64,256]{3,2,0,1:T(8,128)}) fusion(f32[2,64,64,256]{3,2,0,1:T(8,128)S(1)} %bitcast.215, f32[2,64,64,256]{3,2,0,1:T(8,128)} %fusion.34, f32[2,64,64,256]{3,2,0,1:T(8,128)} %copy-done.6), kind=kLoop, calls=%fused_computation.64 | loop fusion | flops 12582912 | bytes 41943040 | tf_op jit(solution)/shard_map/add | solution.py:86
  323.7 6.4 %fusion.45 = f32[64,256,2,64]{1,3,2,0:T(8,128)S(1)} fusion(f32[1,64,64,256]{3,2,0,1:T(8,128)} %get-tuple-element.38, f32[1,64,64,256]{3,2,0,1:T(8,128)} %get-tuple-element.39, f32[1,64,2,64]{3,1,2,0:T(8,128)S(1)} %get-tuple-element.61, f32[1,64,2,64]{3,1,2,0:T(8,128)S(1)} %get-tuple-element.56), kind=kOutput, calls=%fused_computation.87 | convolution fusion | flops 1612726272 | bytes 16842752 | tf_op jit(solution)/shard_map/pjsq,skqc->pkjc/dot_general | solution.py:58
  330.1 4.9 copy.165
  335.0 6.5 %fusion.43 = f32[64,256,2,64]{1,3,2,0:T(8,128)S(1)} fusion(f32[1,64,64,256]{3,2,0,1:T(8,128)} %get-tuple-element.21, f32[1,64,64,256]{3,2,0,1:T(8,128)} %get-tuple-element.20, f32[1,64,2,64]{3,1,2,0:T(8,128)S(1)} %get-tuple-element.61, f32[1,64,2,64]{3,1,2,0:T(8,128)S(1)} %get-tuple-element.56), kind=kOutput, calls=%fused_computation.85 | convolution fusion | flops 1612726272 | bytes 16842752 | tf_op jit(solution)/shard_map/pjsq,skqc->pkjc/dot_general | solution.py:58
  341.4 8.2 %copy.163 = f32[64,256,2,64]{1,0,3,2:T(8,128)} copy(f32[64,256,2,64]{1,3,2,0:T(8,128)S(1)} %fusion.43) | data formatting | bytes 16777216 | tf_op jit(solution)/shard_map/pjsq,skqc->pkjc/dot_general | solution.py:58
  349.6 7.8 %multiply_subtract_fusion = (f32[1,64,64,256]{3,1,2,0:T(8,128)}, f32[1,64,64,256]{3,1,2,0:T(8,128)}, f32[1,64,64,256]{3,1,2,0:T(8,128)S(1)}, f32[1,64,64,256]{3,1,2,0:T(8,128)}) fusion(f32[2,64,64,256]{3,1,2,0:T(8,128)} %bitcast.220, f32[64,64]{0,1:T(8,128)S(1)} %get-tuple-element.64, f32[64,64]{0,1:T(8,128)S(1)} %get-tuple-element.65, ...), kind=kLoop, calls=%fused_computation.62 | loop fusion | flops 12582912 | bytes 33587200 | tf_op jit(solution)/shard_map/sub | solution.py:99
  357.4 5.1 fusion.51
  364.2 5.1 all-to-all-start.1
  369.4 5.3 bitcast_multiply_fusion
  380.1 5.3 all-to-all-done.1
  391.1 4.1 convert_multiply_fusion.1
  395.2 11.6 %bitcast_dynamic-update-slice_fusion.6 = f32[7,128,12288]{1,2,0:T(8,128)} fusion(f32[134,12288]{0,1:T(8,128)} %copy-done, f32[128,4096]{0,1:T(8,128)S(1)} %copy-done.1, f32[128,4096]{0,1:T(8,128)S(1)} %get-tuple-element.40, f32[128,4096]{0,1:T(8,128)S(1)} %get-tuple-element.43), kind=kLoop, calls=%fused_computation.59 | loop fusion | flops 4718591 | bytes 18874368
  406.9 7.4 %bitcast_dynamic-update-slice_fusion.5 = f32[7,128,12288]{1,2,0:T(8,128)} fusion(f32[7,128,12288]{1,2,0:T(8,128)} %bitcast_dynamic-update-slice_fusion.6, f32[134,12288]{0,1:T(8,128)S(1)} %bitcast.213, f32[128,4096]{0,1:T(8,128)S(1)} %copy-done.1, f32[128,4096]{0,1:T(8,128)S(1)} %get-tuple-element.40, f32[128,4096]{0,1:T(8,128)S(1)} %get-tuple-element.43), kind=kLoop, calls=%fused_computation.58 | loop fusion | flops 4718592 | bytes 18874368
  414.3 7.5 %bitcast_dynamic-update-slice_fusion.4 = f32[7,128,12288]{1,2,0:T(8,128)} fusion(f32[7,128,12288]{1,2,0:T(8,128)} %bitcast_dynamic-update-slice_fusion.5, f32[134,12288]{0,1:T(8,128)S(1)} %bitcast.213, f32[128,4096]{0,1:T(8,128)S(1)} %copy-done.1, f32[128,4096]{0,1:T(8,128)S(1)} %get-tuple-element.40, f32[128,4096]{0,1:T(8,128)S(1)} %get-tuple-element.43), kind=kLoop, calls=%fused_computation.57 | loop fusion | flops 4718592 | bytes 18874368
  421.7 7.3 %bitcast_dynamic-update-slice_fusion.3 = f32[7,128,12288]{1,2,0:T(8,128)} fusion(f32[7,128,12288]{1,2,0:T(8,128)} %bitcast_dynamic-update-slice_fusion.4, f32[134,12288]{0,1:T(8,128)S(1)} %bitcast.213, f32[128,4096]{0,1:T(8,128)S(1)} %copy-done.1, f32[128,4096]{0,1:T(8,128)S(1)} %get-tuple-element.40, f32[128,4096]{0,1:T(8,128)S(1)} %get-tuple-element.43), kind=kLoop, calls=%fused_computation.56 | loop fusion | flops 4718592 | bytes 18874368
  429.1 7.3 %bitcast_dynamic-update-slice_fusion.2 = f32[7,128,12288]{1,2,0:T(8,128)} fusion(f32[7,128,12288]{1,2,0:T(8,128)} %bitcast_dynamic-update-slice_fusion.3, f32[134,12288]{0,1:T(8,128)S(1)} %bitcast.213, f32[128,4096]{0,1:T(8,128)S(1)} %copy-done.1, f32[128,4096]{0,1:T(8,128)S(1)} %get-tuple-element.40, f32[128,4096]{0,1:T(8,128)S(1)} %get-tuple-element.43), kind=kLoop, calls=%fused_computation.55 | loop fusion | flops 4718592 | bytes 18874368
  436.4 7.3 %bitcast_dynamic-update-slice_fusion.1 = f32[7,128,12288]{1,2,0:T(8,128)} fusion(f32[7,128,12288]{1,2,0:T(8,128)} %bitcast_dynamic-update-slice_fusion.2, f32[134,12288]{0,1:T(8,128)S(1)} %bitcast.213, f32[128,4096]{0,1:T(8,128)S(1)} %copy-done.1, f32[128,4096]{0,1:T(8,128)S(1)} %get-tuple-element.40, f32[128,4096]{0,1:T(8,128)S(1)} %get-tuple-element.43), kind=kLoop, calls=%fused_computation.54 | loop fusion | flops 4718592 | bytes 18874368
  443.7 7.4 %bitcast_dynamic-update-slice_fusion = f32[7,128,12288]{1,2,0:T(8,128)} fusion(f32[7,128,12288]{1,2,0:T(8,128)} %bitcast_dynamic-update-slice_fusion.1, f32[134,12288]{0,1:T(8,128)S(1)} %bitcast.213, f32[128,4096]{0,1:T(8,128)S(1)} %copy-done.1, f32[128,4096]{0,1:T(8,128)S(1)} %get-tuple-element.40, f32[128,4096]{0,1:T(8,128)S(1)} %get-tuple-element.43), kind=kLoop, calls=%fused_computation.53 | loop fusion | flops 4718592 | bytes 18874368 | tf_op jit(solution)/shard_map/stack | solution.py:164
  451.1 21.1 %reduce_sum.30 = bf16[7,12288]{1,0:T(8,128)(2,1)} reduce(f32[7,128,12288]{1,2,0:T(8,128)} %bitcast_dynamic-update-slice_fusion, f32[]{:T(128)} %constant.56.clone.1), dimensions={1}, to_apply=%region_0.1 | reduce | flops 10924032 | bytes 44212228 | tf_op jit(solution)/shard_map/reduce_sum | solution.py:163
  472.3 6.3 %pad_maximum_fusion.1 = bf16[128,12288]{0,1:T(8,128)(2,1)} fusion(f32[128,4096]{0,1:T(8,128)} %get-tuple-element.41, f32[128,4096]{0,1:T(8,128)S(1)} %get-tuple-element.40, f32[128,4096]{0,1:T(8,128)} %copy-done.3), kind=kLoop, calls=%fused_computation.52 | loop fusion | flops 9437184 | bytes 9437184 | tf_op jit(solution)/shard_map/concatenate | solution.py:154
  495.6 12.4 %pad_maximum_fusion = f32[134,12288]{0,1:T(8,128)} fusion(f32[6,12288]{0,1:T(8,128)} %copy.94, f32[128,4096]{0,1:T(8,128)} %get-tuple-element.41, f32[128,4096]{0,1:T(8,128)S(1)} %get-tuple-element.40, f32[128,4096]{0,1:T(8,128)} %copy-done.3), kind=kLoop, calls=%fused_computation | loop fusion | flops 4939776 | bytes 13172736 | tf_op jit(solution)/shard_map/concatenate | solution.py:156
  508.1 32.3 %fusion.46 = bf16[1,128,12288]{1,2,0:T(8,128)(2,1)} fusion(f32[134,12288]{0,1:T(8,128)} %pad_maximum_fusion, f32[12288]{0:T(1024)S(1)} %bitcast.248, f32[12288]{0:T(1024)S(1)} %bitcast.250, f32[12288]{0:T(1024)S(1)} %bitcast.240, f32[12288]{0:T(1024)S(1)} %bitcast.242, f32[12288]{0:T(1024)S(1)} %bitcast.244, f32[12288]{0:T(1024)S(1)} %bitcast.246, ...), kind=kLoop, calls=%fused_computation.89 | loop fusion | flops 25165824 | bytes 47529984 | tf_op jit(solution)/shard_map/broadcast_in_dim | solution.py:176
  540.4 4.6 copy.99
  (115 shorter events, 68.6 us)
Async XLA Ops:
  7.2 13.8 %copy-start.25 = (f32[1,7,12288]{2,0,1:T(1,128)S(1)}, f32[1,7,12288]{2,0,1:T(1,128)}, u32[]{:S(2)}) copy-start(f32[1,7,12288]{2,0,1:T(1,128)} %param.7) | copy-start | bytes 1032196
  9.5 143.3 %collective-permute-start.2 = (bf16[1,128,4096]{1,2,0:T(8,128)(2,1)}, bf16[1,128,4096]{1,2,0:T(8,128)(2,1)S(1)}, u32[]{:S(2)}, u32[]{:S(2)}) collective-permute-start(bf16[1,128,4096]{1,2,0:T(8,128)(2,1)} %copy.84), channel_id=1, source_target_pairs={{0,112},{16,0},{32,16},{48,32},{64,48},{80,64},{96,80},{112,96},{1... | collective-permute-start | bytes 3145736 | tf_op jit(solution)/shard_map/ppermute | solution.py:11
  14.1 104.1 %copy-start.10 = (bf16[1,256,2048]{2,1,0:T(8,128)(2,1)S(1)}, bf16[1,256,2048]{2,1,0:T(8,128)(2,1)}, u32[]{:S(2)}) copy-start(bf16[1,256,2048]{2,1,0:T(8,128)(2,1)} %param.8) | copy-start | bytes 3145732
  14.1 91.8 %collective-permute-start = (bf16[1,128,12288]{1,2,0:T(8,128)(2,1)}, bf16[1,128,12288]{1,2,0:T(8,128)(2,1)}, u32[]{:S(2)}, u32[]{:S(2)}) collective-permute-start(bf16[1,128,12288]{1,2,0:T(8,128)(2,1)} %copy.69), channel_id=1, source_target_pairs={{0,16},{16,32},{32,48},{48,64},{64,80},{80,96},{96,112},{112,0},{1... | collective-permute-start | bytes 9437192 | tf_op jit(solution)/shard_map/ppermute | solution.py:11
  21.7 106.5 %copy-start.11 = (f32[1,1,12288]{2,0,1:T(1,128)}, f32[1,1,12288]{2,0,1:T(1,128)S(1)}, u32[]{:S(2)}) copy-start(f32[1,1,12288]{2,0,1:T(1,128)S(1)} %get-tuple-element.45) | copy-start | bytes 147460
  113.3 6.5 %collective-permute-start.1 = (bf16[6,12288]{1,0:T(8,128)(2,1)}, bf16[6,12288]{1,0:T(8,128)(2,1)}, u32[]{:S(2)}, u32[]{:S(2)}) collective-permute-start(bf16[6,12288]{1,0:T(8,128)(2,1)} %copy.70), channel_id=1, source_target_pairs={{0,1},{1,2},{2,3},{3,4},{4,5},{5,6},{6,7},{7,8},{8,9},{9,10},{10,1... | collective-permute-start | bytes 442376 | tf_op jit(solution)/shard_map/ppermute | solution.py:17
  123.4 4.8 copy-start.13
  123.4 4.8 copy-start.15
  123.5 4.8 copy-start.17
  123.5 4.8 copy-start.19
  123.5 4.8 copy-start.21
  123.5 4.8 copy-start.23
  128.2 24.6 %copy-start = (f32[134,12288]{0,1:T(8,128)}, f32[134,12288]{0,1:T(8,128)S(1)}, u32[]{:S(2)}) copy-start(f32[134,12288]{0,1:T(8,128)S(1)} %maximum_convert_fusion) | copy-start | bytes 19759108
  152.8 11.3 %copy-start.9 = (bf16[1,128,4096]{1,2,0:T(8,128)(2,1)}, bf16[1,128,4096]{1,2,0:T(8,128)(2,1)S(1)}, u32[]{:S(2)}) copy-start(bf16[1,128,4096]{1,2,0:T(8,128)(2,1)S(1)} %collective-permute-done.2) | copy-start | bytes 3145732
  156.0 22.7 %all-to-all-start.2 = ((bf16[128,16,256]{0,2,1:T(8,128)(2,1)}), bf16[128,16,256]{0,2,1:T(8,128)(2,1)S(1)}, u32[]{:S(2)}, u32[]{:S(2)}) async-start(bf16[128,16,256]{0,2,1:T(8,128)(2,1)} %bitcast.235), calls=%async_computation.2 | async-start | bytes 2097152 | tf_op jit(solution)/shard_map/all_to_all | solution.py:141
  179.2 2.6 slice-start.5
  180.5 2.4 slice-start.6
  206.9 8.7 %copy-start.5 = (f32[2,64,64,256]{3,2,0,1:T(8,128)}, f32[2,64,64,256]{3,2,0,1:T(8,128)S(1)}, u32[]{:S(2)}) copy-start(f32[2,64,64,256]{3,2,0,1:T(8,128)S(1)} %fusion.40) | copy-start | bytes 25165828
  215.6 5.8 %copy-start.6 = (f32[2,64,64,256]{3,2,0,1:T(8,128)}, f32[2,64,64,256]{3,2,0,1:T(8,128)S(1)}, u32[]{:S(2)}) copy-start(f32[2,64,64,256]{3,2,0,1:T(8,128)S(1)} %fusion.37) | copy-start | bytes 25165828
  237.2 4.5 copy-start.27
  264.9 1.0 copy-start.7
  288.3 2.6 copy-start.8
  293.7 18.1 %slice-start.3 = ((s8[8388608]{0:T(1024)(128)(4,1)}), s8[4194304]{0:T(1024)(128)(4,1)S(1)}, s32[]{:S(2)}) async-start(s8[8388608]{0:T(1024)(128)(4,1)} %bitcast.214), calls=%async_computation.8 | async-start | bytes 8388608
  297.8 14.0 %slice-start.4 = ((s8[8388608]{0:T(1024)(128)(4,1)}), s8[4194304]{0:T(1024)(128)(4,1)S(1)}, s32[]{:S(2)}) async-start(s8[8388608]{0:T(1024)(128)(4,1)} %bitcast.214), calls=%async_computation.9 | async-start | bytes 8388608
  364.2 21.2 %all-to-all-start.1 = ((bf16[16,128,256]{2,1,0:T(8,128)(2,1)}), bf16[16,128,256]{2,1,0:T(8,128)(2,1)}, u32[]{:S(2)}, u32[]{:S(2)}) async-start(bf16[16,128,256]{2,1,0:T(8,128)(2,1)} %bitcast.234), calls=%async_computation.1 | async-start | bytes 2097152 | tf_op jit(solution)/shard_map/all_to_all | solution.py:140
  369.3 175.7 %all-gather.4.cloned.1.call-start = ((), (), s32[]{:S(2)}) async-start(), calls=%async_computation.4 | async-start | bytes 3342336 | tf_op jit(solution)/shard_map/all_gather | solution.py:173
  377.2 13.9 %copy-start.26 = (f32[1,4096]{1,0:T(1,128)S(1)}, f32[1,4096]{1,0:T(1,128)}, u32[]{:S(2)}) copy-start(f32[1,4096]{1,0:T(1,128)} %param.9) | copy-start | bytes 49156
  391.1 4.1 copy-start.1
  391.1 15.8 %slice-start = ((s8[12582912]{0:T(1024)(128)(4,1)}), s8[4194304]{0:T(1024)(128)(4,1)S(1)}, s32[]{:S(2)}) async-start(s8[12582912]{0:T(1024)(128)(4,1)} %bitcast.212), calls=%async_computation.5 | async-start | bytes 8388608
  391.1 15.8 %slice-start.1 = ((s8[12582912]{0:T(1024)(128)(4,1)}), s8[4194304]{0:T(1024)(128)(4,1)S(1)}, s32[]{:S(2)}) async-start(s8[12582912]{0:T(1024)(128)(4,1)} %bitcast.212), calls=%async_computation.6 | async-start | bytes 8388608
  395.2 48.5 %copy-start.3 = (f32[128,4096]{0,1:T(8,128)}, f32[128,4096]{0,1:T(8,128)S(1)}, u32[]{:S(2)}) copy-start(f32[128,4096]{0,1:T(8,128)S(1)} %get-tuple-element.43) | copy-start | bytes 6291460
  395.2 11.7 %slice-start.2 = ((s8[12582912]{0:T(1024)(128)(4,1)}), s8[4194304]{0:T(1024)(128)(4,1)S(1)}, s32[]{:S(2)}) async-start(s8[12582912]{0:T(1024)(128)(4,1)} %bitcast.212), calls=%async_computation.7 | async-start | bytes 8388608
  481.8 10.2 %collective-permute-start.3 = (bf16[6,12288]{1,0:T(8,128)(2,1)S(1)}, bf16[6,12288]{1,0:T(8,128)(2,1)S(1)}, u32[]{:S(2)}, u32[]{:S(2)}) collective-permute-start(bf16[6,12288]{1,0:T(8,128)(2,1)S(1)} %copy.93), channel_id=1, source_target_pairs={{1,0},{2,1},{3,2},{4,3},{5,4},{6,5},{7,6},{8,7},{9,8},{10,9},{11,1... | collective-permute-start | bytes 442376 | tf_op jit(solution)/shard_map/ppermute | solution.py:17
  495.6 12.4 %copy-start.2 = (f32[128,4096]{0,1:T(8,128)S(1)}, f32[128,4096]{0,1:T(8,128)}, u32[]{:S(2)}) copy-start(f32[128,4096]{0,1:T(8,128)} %get-tuple-element.41) | copy-start | bytes 6291460
  495.6 12.4 %copy-start.4 = (f32[128,4096]{0,1:T(8,128)S(1)}, f32[128,4096]{0,1:T(8,128)}, u32[]{:S(2)}) copy-start(f32[128,4096]{0,1:T(8,128)} %copy-done.3) | copy-start | bytes 6291460
  495.6 12.4 %copy-start.12 = (f32[1,1,12288]{2,0,1:T(1,128)S(1)}, f32[1,1,12288]{2,0,1:T(1,128)}, u32[]{:S(2)}) copy-start(f32[1,1,12288]{2,0,1:T(1,128)} %copy-done.11) | copy-start | bytes 147460
  495.6 12.4 %copy-start.14 = (f32[1,1,12288]{2,0,1:T(1,128)S(1)}, f32[1,1,12288]{2,0,1:T(1,128)}, u32[]{:S(2)}) copy-start(f32[1,1,12288]{2,0,1:T(1,128)} %get-tuple-element.46) | copy-start | bytes 147460
  495.6 12.4 %copy-start.16 = (f32[1,1,12288]{2,0,1:T(1,128)S(1)}, f32[1,1,12288]{2,0,1:T(1,128)}, u32[]{:S(2)}) copy-start(f32[1,1,12288]{2,0,1:T(1,128)} %get-tuple-element.47) | copy-start | bytes 147460
  495.6 12.4 %copy-start.18 = (f32[1,1,12288]{2,0,1:T(1,128)S(1)}, f32[1,1,12288]{2,0,1:T(1,128)}, u32[]{:S(2)}) copy-start(f32[1,1,12288]{2,0,1:T(1,128)} %get-tuple-element.48) | copy-start | bytes 147460
  495.6 12.4 %copy-start.20 = (f32[1,1,12288]{2,0,1:T(1,128)S(1)}, f32[1,1,12288]{2,0,1:T(1,128)}, u32[]{:S(2)}) copy-start(f32[1,1,12288]{2,0,1:T(1,128)} %get-tuple-element.49) | copy-start | bytes 147460
  495.6 12.4 %copy-start.22 = (f32[1,1,12288]{2,0,1:T(1,128)S(1)}, f32[1,1,12288]{2,0,1:T(1,128)}, u32[]{:S(2)}) copy-start(f32[1,1,12288]{2,0,1:T(1,128)} %get-tuple-element.50) | copy-start | bytes 147460
  495.6 12.4 %copy-start.24 = (f32[1,1,12288]{2,0,1:T(1,128)S(1)}, f32[1,1,12288]{2,0,1:T(1,128)}, u32[]{:S(2)}) copy-start(f32[1,1,12288]{2,0,1:T(1,128)} %get-tuple-element.51) | copy-start | bytes 147460
Sparse Core Ops, SparseCore 0:
  472.4 35.2 all-gather.3
